TPU v7x, 128 devices: a whole 4x4x4 slice. The times are simulated.
128 devices in a mesh: req: 16 (over x, y), row: 8 (over z, core).
Axes of the slice: x: 4, y: 4, z: 4, core: 2. Of those that a mesh axis runs over, the one named last changes fastest.
Arguments:
- patches: bfloat16 [8, 2048, 1280], P('row', 'req'), may hold values from -6 to 6
- picture_ids: int32 [8, 2048], P('row'), may hold values from -1 to 15, as said below
- ln_attn: float32 [1280], replicated, may hold values from 0.1 to 1.9
- w_qkv: bfloat16 [3, 1280, 1280], P(None, None, 'req'), may hold values from -6 to 6
- w_out: bfloat16 [1280, 1280], P('req'), may hold values from -1.25 to 1.25
- ln_mlp: float32 [1280], replicated, may hold values from 0.1 to 1.9
- w_up: bfloat16 [1280, 5120], P(None, 'req'), may hold values from -0.15625 to 0.15625
- w_down: bfloat16 [5120, 1280], P('req'), may hold values from -0.3125 to 0.3125
- w_merge: bfloat16 [5120, 1280], replicated, may hold values from -0.078125 to 0.078125
- text_embed: bfloat16 [16384, 1280], P(('req', 'row')), may hold values from -6 to 6
- slot_dest: int32 [8, 512], P('row', 'req'), may hold values from -1 to 16383, as said below
Outputs:
- prompt_embed: bfloat16 [16384, 1280], P(('req', 'row'))
Inputs may be any that keep to these rules, and one draw needn't show every extreme that they name: `picture_ids`: each group holds whole pictures one after another from its first row, each picture's length a multiple of 4 and laid out so that every aligned run of four rows is one 2x2 window; rows after the last picture are padding. `slot_dest`: A merged row has a prompt row exactly when its patch rows belong to a picture; no prompt row is named twice; a merged row of group g (rows of the row index g) names a prompt row of a device with the same row index; at most 2 merged rows of one device name prompt rows of one device, and in every draw some device sends that many to one device.
All inputs are finite; a program needn't handle non-finite values.
Results may differ from a plain program's by a relative error of at most 0.023.
Values may be sent and summed in bfloat16 or wider, within the bound.
No kernel may reach another device: no remote copies, remote signals or barrier semaphores. Data moves between devices by JAX's collectives and lax.ppermute only.
A program may use at most 128 MiB of HBM per device.

v0:
```python
import math
import jax
import jax.numpy as jnp
from jax import lax
from jax.sharding import PartitionSpec as P

HEAD = 80


def layer_norm(rows, gain):
    rows32 = rows.astype(jnp.float32)
    center = rows32 - jnp.mean(rows32, axis=-1, keepdims=True)
    spread = jnp.mean(center * center, axis=-1, keepdims=True)
    return center * lax.rsqrt(spread + 1e-06) * gain


def local(
    patches,
    picture_ids,
    ln_attn,
    w_qkv,
    w_out,
    ln_mlp,
    w_up,
    w_down,
    w_merge,
    text_embed,
    slot_dest,
):
    rows = patches[0]
    local_rows = rows.shape[0]
    width = rows.shape[1]
    ids = picture_ids[0]
    group_rows = ids.shape[0]
    head_cols = w_out.shape[0]
    req_count = lax.axis_size("req")
    row_count = lax.axis_size("row")
    normed = layer_norm(rows, ln_attn).astype(jnp.bfloat16)
    qkv = jnp.einsum(
        "rd,tdc->trc",
        lax.all_gather(normed, "req", axis=0, tiled=True),
        w_qkv,
        preferred_element_type=jnp.float32,
    ).astype(jnp.bfloat16)
    keys = qkv[1]
    values = qkv[2]
    block = min(512, group_rows)
    blocks = group_rows // block
    scale = 1.0 / math.sqrt(HEAD)

    def attend(item):
        query_block, id_block = item
        same = id_block[:, None] == ids[None, :]
        scores = (
            jnp.einsum("qc,kc->qk", query_block, keys, preferred_element_type=jnp.float32) * scale
        )
        scores = jnp.where(same, scores, -1e30)
        top = jnp.max(scores, axis=1, keepdims=True)
        expo = jnp.exp(scores - top)
        probs = (expo / jnp.sum(expo, axis=1, keepdims=True)).astype(jnp.bfloat16)
        results = [jnp.dot(probs, values, preferred_element_type=jnp.float32).astype(jnp.bfloat16)]
        return jnp.concatenate(results, axis=1)

    attended = lax.map(
        attend, (qkv[0].reshape(blocks, block, head_cols), ids.reshape(blocks, block))
    )
    attended = attended.reshape(group_rows, head_cols)
    piece = lax.slice_in_dim(attended, 0, local_rows * lax.axis_size("req"), axis=0)
    attn = lax.psum_scatter(
        jnp.dot(piece, w_out, preferred_element_type=jnp.float32).astype(jnp.bfloat16),
        "req",
        scatter_dimension=0,
        tiled=True,
    ).astype(jnp.float32)
    resid = (rows.astype(jnp.float32) + attn).astype(jnp.bfloat16)
    normed_two = layer_norm(resid, ln_mlp).astype(jnp.bfloat16)
    hidden = jax.nn.gelu(
        jnp.dot(
            lax.all_gather(normed_two, "req", axis=0, tiled=True),
            w_up,
            preferred_element_type=jnp.float32,
        ),
        approximate=False,
    ).astype(jnp.bfloat16)
    piece = lax.slice_in_dim(hidden, 0, local_rows * lax.axis_size("req"), axis=0)
    mlp = lax.psum_scatter(
        jnp.dot(piece, w_down, preferred_element_type=jnp.float32).astype(jnp.bfloat16),
        "req",
        scatter_dimension=0,
        tiled=True,
    ).astype(jnp.float32)
    vision = (resid.astype(jnp.float32) + mlp).astype(jnp.bfloat16)
    merged = vision.reshape(local_rows // 4, 4 * width)
    merged_count = merged.shape[0]
    dest = slot_dest[0]
    prompt_rows = text_embed.shape[0]
    slot_cap = max(2, merged_count // req_count)
    owner = jnp.where(dest >= 0, dest // prompt_rows // row_count, -1)
    order = jnp.arange(merged_count)
    same_owner = (owner[:, None] == owner[None, :]) & (order[None, :] < order[:, None])
    ranks = jnp.sum(same_owner.astype(jnp.int32), axis=1)
    target = jnp.where(owner >= 0, owner * slot_cap + ranks, -1)
    select = target[None, :] == jnp.arange(req_count * slot_cap)[:, None]
    places = jnp.sum(jnp.where(select, (dest % prompt_rows + 1)[None, :], 0), axis=1) - 1
    chooser = select.astype(jnp.bfloat16)
    outgoing = jnp.dot(chooser, merged, preferred_element_type=jnp.float32).astype(jnp.bfloat16)
    arrived, landing = (
        lax.all_to_all(
            outgoing.reshape(req_count, slot_cap, -1),
            "req",
            split_axis=0,
            concat_axis=0,
            tiled=True,
        ),
        lax.all_to_all(
            places.reshape(req_count, slot_cap), "req", split_axis=0, concat_axis=0, tiled=True
        ),
    )
    arrived = arrived.reshape(req_count * slot_cap, -1)
    landing = landing.reshape(-1)
    incoming = jnp.dot(arrived, w_merge, preferred_element_type=jnp.float32).astype(jnp.bfloat16)
    placer = landing[None, :] == jnp.arange(prompt_rows)[:, None]
    placed = jnp.dot(
        placer.astype(jnp.bfloat16), incoming, preferred_element_type=jnp.float32
    ).astype(jnp.bfloat16)
    filled = jnp.any(placer, axis=1)
    return jnp.where(filled[:, None], placed, text_embed)


def solution(mesh):
    return jax.shard_map(
        local,
        mesh=mesh,
        in_specs=(
            P("row", "req", None),
            P("row", None),
            P(),
            P(None, None, "req"),
            P("req", None),
            P(),
            P(None, "req"),
            P("req", None),
            P(),
            P(("req", "row"), None),
            P("row", "req"),
        ),
        out_specs=P(("req", "row"), None),
        check_vma=False,
    )
```

profile of v0, /device:TPU:0, one launch (start us, length us, event | category | flops | bytes accessed | tf_op | source)
XLA Modules:
  0.0 349.8 jit_solution(17088282344082328541)
XLA Ops:
  6.5 1.2 convert_reduce_fusion.1
  7.7 1.2 fusion.59
  8.9 1.9 fusion.61
  11.5 1.4 reduce.7
  12.9 56.8 %all-gather.3.cloned.1.call-done = bf16[2048,1280]{1,0:T(8,128)(2,1)} async-done(((bf16[128,1280]{1,0:T(8,128)(2,1)}), bf16[2048,1280]{1,0:T(8,128)(2,1)}) %all-gather.3.cloned.1.call-update) | async-done | bytes 5242896 | tf_op jit(solution)/shard_map/all_gather | solution.py:41
  69.8 4.2 %fusion.105 = f32[2048,240]{0,1:S(1)} fusion(bf16[2048,1280]{1,0:T(8,128)(2,1)} %all-gather.3.cloned.1.call-done, bf16[1280,240]{0,1:T(8,128)(2,1)} %bitcast.94), kind=kOutput, calls=%fused_computation.160 | convolution fusion | flops 1258291200 | bytes 7823360
  75.0 11.0 %while.10 = (s32[]{:T(128)}, bf16[4,512,80]{1,2,0:T(8,128)(2,1)S(1)}, s32[4,512]{1,0:T(4,128)S(1)}, s32[1,2048]{1,0:T(1,128)S(1)}, bf16[4,512,80]{2,1,0:T(8,128)...) while((s32[]{:T(128)}, bf16[4,512,80]{1,2,0:T(8,128)(2,1)S(1)}, ...), condition=%wide.region_8.9_spmd, body=%wide.region_5.8_spmd.sunk | while | flops 345021440 | bytes 13869153 | solution.py:64
  75.1 0.9 fusion.125
  76.7 1.1 fusion.127
  79.4 1.1 fusion.127
  82.2 1.1 fusion.127
  84.9 1.1 fusion.127
  86.1 3.9 %convolution_convert_fusion.1 = bf16[2048,1280]{1,0:T(8,128)(2,1)} fusion(bf16[2048,80]{0,1:T(8,128)(2,1)S(1)} %bitcast.88, bf16[80,1280]{1,0:T(8,128)(2,1)S(1)} %copy-done.3), kind=kOutput, calls=%fused_computation.13 | convolution fusion | flops 422051840 | bytes 5775360 | tf_op jit(solution)/shard_map/dot_general | solution.py:70
  90.0 78.7 %reduce-scatter.3.cloned.1.call-done = bf16[128,1280]{1,0:T(8,128)(2,1)} async-done(((bf16[2048,1280]{1,0:T(8,128)(2,1)}), bf16[128,1280]{1,0:T(8,128)(2,1)}) %reduce-scatter.3.cloned.1.call-update) | async-done | bytes 327696 | tf_op jit(solution)/shard_map/reduce_scatter | solution.py:69
  168.8 1.2 convert_reduce_fusion
  170.2 1.0 fusion.58
  171.4 55.5 %all-gather.5.cloned.1.call-done = bf16[2048,1280]{1,0:T(8,128)(2,1)} async-done(((bf16[128,1280]{1,0:T(8,128)(2,1)}), bf16[2048,1280]{1,0:T(8,128)(2,1)}) %all-gather.5.cloned.1.call-update) | async-done | bytes 5242896 | tf_op jit(solution)/shard_map/all_gather | solution.py:79
  226.9 13.4 %convolution_convert_fusion = bf16[2048,1280]{1,0:T(8,128)(2,1)} fusion(bf16[320,1280]{1,0:T(8,128)(2,1)S(1)} %copy-done, bf16[2048,1280]{1,0:T(8,128)(2,1)} %all-gather.5.cloned.1.call-done, bf16[1280,320]{0,1:T(8,128)(2,1)S(1)} %copy-done.6), kind=kOutput, calls=%fused_computation.12 | convolution fusion | flops 3400663040 | bytes 12124160 | tf_op jit(solution)/shard_map/dot_general | solution.py:87
  242.0 5.3 %all-to-all-start = ((s32[16,1,2]{2,1,0:T(1,128)}), s32[16,1,2]{2,1,0:T(1,128)S(1)}, u32[]{:S(2)}, u32[]{:S(2)}) async-start(s32[16,1,2]{2,1,0:T(1,128)} %bitcast.9), calls=%async_computation | async-start | bytes 16384 | tf_op jit(solution)/shard_map/all_to_all | solution.py:115
  247.3 71.8 %reduce-scatter.5.cloned.1.call-done = bf16[128,1280]{1,0:T(8,128)(2,1)} async-done(((bf16[2048,1280]{1,0:T(8,128)(2,1)}), bf16[128,1280]{1,0:T(8,128)(2,1)}) %reduce-scatter.5.cloned.1.call-update) | async-done | bytes 327696 | tf_op jit(solution)/shard_map/reduce_scatter | solution.py:86
  319.1 1.0 fusion.63
  321.4 4.9 %all-to-all-start.1 = ((bf16[16,2,5120]{2,1,0:T(2,128)(2,1)}), bf16[16,2,5120]{2,1,0:T(2,128)(2,1)S(1)}, u32[]{:S(2)}, u32[]{:S(2)}) async-start(bf16[16,2,5120]{2,1,0:T(2,128)(2,1)} %reshape.113), calls=%async_computation.3 | async-start | bytes 655360 | tf_op jit(solution)/shard_map/all_to_all | solution.py:108
  327.2 7.9 %all-to-all-done.1 = bf16[16,2,5120]{2,1,0:T(2,128)(2,1)S(1)} async-done(((bf16[16,2,5120]{2,1,0:T(2,128)(2,1)}), bf16[16,2,5120]{2,1,0:T(2,128)(2,1)S(1)}, u32[]{:S(2)}, u32[]{:S(2)}) %all-to-all-start.1) | async-done | bytes 327712 | tf_op jit(solution)/shard_map/all_to_all | solution.py:108
  335.3 8.0 %fusion.18 = bf16[128,1280]{1,0:T(8,128)(2,1)} fusion(bf16[128,1280]{1,0:T(8,128)(2,1)S(1)} %copy-done.2, bf16[32,5120]{1,0:T(8,128)(2,1)S(1)} %reshape.114, bf16[5120,1280]{1,0:T(8,128)(2,1)} %param.21, pred[128]{0:T(512)(128)(4,1)S(1)} %fusion.64, s32[32]{0:T(128)S(1)} %eq.69), kind=kOutput, calls=%fused_computation.35 | convolution fusion | flops 430288896 | bytes 14090496 | tf_op jit(solution)/shard_map/dot_general | solution.py:123
  (64 shorter events, 11.8 us)
Async XLA Ops:
  6.5 220.4 %copy-start = (bf16[320,1280]{1,0:T(8,128)(2,1)S(1)}, bf16[320,1280]{1,0:T(8,128)(2,1)}, u32[]{:S(2)}) copy-start(bf16[320,1280]{1,0:T(8,128)(2,1)} %param.20) | copy-start | bytes 2457604
  6.5 63.2 %all-gather.3.cloned.1.call-start = ((), (), s32[]{:S(2)}) async-start(), calls=%async_computation.4 | async-start | bytes 5570560 | tf_op jit(solution)/shard_map/all_gather | solution.py:41
  10.9 157.9 %reduce-scatter.3.cloned.1.call-start = ((), (), s32[]{:S(2)}) async-start(), calls=%async_computation.5 | async-start | bytes 5570560 | tf_op jit(solution)/shard_map/reduce_scatter | solution.py:69
  74.1 0.9 copy-start.4
  75.0 11.0 %copy-start.3 = (bf16[80,1280]{1,0:T(8,128)(2,1)S(1)}, bf16[80,1280]{1,0:T(8,128)(2,1)}, u32[]{:S(2)}) copy-start(bf16[80,1280]{1,0:T(8,128)(2,1)} %param.17) | copy-start | bytes 614404
  90.0 78.8 %copy-start.1 = (bf16[1,128,1280]{2,1,0:T(8,128)(2,1)S(1)}, bf16[1,128,1280]{2,1,0:T(8,128)(2,1)}, u32[]{:S(2)}) copy-start(bf16[1,128,1280]{2,1,0:T(8,128)(2,1)} %param.13) | copy-start | bytes 983044
  90.0 80.2 %copy-start.5 = (f32[1280]{0:T(1024)S(1)}, f32[1280]{0:T(1024)}, u32[]{:S(2)}) copy-start(f32[1280]{0:T(1024)} %param.18) | copy-start | bytes 15364
  90.0 137.0 %copy-start.6 = (bf16[1280,320]{0,1:T(8,128)(2,1)S(1)}, bf16[1280,320]{0,1:T(8,128)(2,1)}, u32[]{:S(2)}) copy-start(bf16[1280,320]{0,1:T(8,128)(2,1)} %param.19) | copy-start | bytes 2457604
  90.0 136.9 %all-gather.5.cloned.1.call-start = ((), (), s32[]{:S(2)}) async-start(), calls=%async_computation.6 | async-start | bytes 5570560 | tf_op jit(solution)/shard_map/all_gather | solution.py:79
  171.2 147.9 %reduce-scatter.5.cloned.1.call-start = ((), (), s32[]{:S(2)}) async-start(), calls=%async_computation.7 | async-start | bytes 5570560 | tf_op jit(solution)/shard_map/reduce_scatter | solution.py:86
  240.3 0.7 copy-start.7
  241.0 94.3 %copy-start.2 = (bf16[128,1280]{1,0:T(8,128)(2,1)S(1)}, bf16[128,1280]{1,0:T(8,128)(2,1)}, u32[]{:S(2)}) copy-start(bf16[128,1280]{1,0:T(8,128)(2,1)} %param.22) | copy-start | bytes 983044
  242.0 79.4 %all-to-all-start = ((s32[16,1,2]{2,1,0:T(1,128)}), s32[16,1,2]{2,1,0:T(1,128)S(1)}, u32[]{:S(2)}, u32[]{:S(2)}) async-start(s32[16,1,2]{2,1,0:T(1,128)} %bitcast.9), calls=%async_computation | async-start | bytes 16384 | tf_op jit(solution)/shard_map/all_to_all | solution.py:115
  321.4 13.8 %all-to-all-start.1 = ((bf16[16,2,5120]{2,1,0:T(2,128)(2,1)}), bf16[16,2,5120]{2,1,0:T(2,128)(2,1)S(1)}, u32[]{:S(2)}, u32[]{:S(2)}) async-start(bf16[16,2,5120]{2,1,0:T(2,128)(2,1)} %reshape.113), calls=%async_computation.3 | async-start | bytes 655360 | tf_op jit(solution)/shard_map/all_to_all | solution.py:108
Sparse Core Ops, SparseCore 0:
  11.0 58.7 all-gather.2
  90.1 78.6 reduce-scatter.2
  171.3 55.5 all-gather.4
  240.5 78.5 reduce-scatter.4
where the time goes:
time: 350 us
  waiting for transfers between devices  271 us (77%)
  matrix products  37.6 us (11%)
  between operations  13.3 us (4%)
  other arithmetic  13.2 us (4%)
  starting transfers between devices  10.5 us (3%)
  local copies, waits for them, and re-layouts  4.15 us (1%)
    reduce_scatter x1, waiting for transfers between devices, local(): lax.psum_scatter(jnp.dot(piece, w_out, preferred_element_type=jnp.float32...  78.7 us
    reduce_scatter x1, waiting for transfers between devices, local(): lax.psum_scatter(jnp.dot(piece, w_down, preferred_element_type=jnp.float3...  71.8 us
    all_gather x1, waiting for transfers between devices, local(): lax.all_gather(normed, 'req', axis=0, tiled=True)  56.8 us
    all_gather x1, waiting for transfers between devices, local(): lax.all_gather(normed_two, 'req', axis=0, tiled=True)  55.5 us
    dot_general x1, matrix products, local(): jnp.dot(piece, w_down, preferred_element_type=jnp.float32)  13.4 us
    dot_general x1, matrix products, local(): jnp.dot(placer.astype(jnp.bfloat16), incoming, preferred_element_type=jnp...  7.96 us
    all_to_all x1, waiting for transfers between devices, local(): lax.all_to_all(outgoing.reshape(req_count, slot_cap, -1), 'req', split_ax...  7.94 us
  transfers between devices with their start and end apart: 6, of which 5 were waited for; matrix products, arithmetic and copies ran while one was open for 2% of the time, Pallas kernels for 0%

commit v1 on v0

--- a/solution.py
+++ b/solution.py
@@ -5,6 +5,28 @@
 from jax.sharding import PartitionSpec as P
 
 HEAD = 80
+
+
+def joined_along(pieces, dim):
+    lengths = list(pieces.shape[1:])
+    lengths[dim] *= pieces.shape[0]
+    return jnp.moveaxis(pieces, 0, dim).reshape(lengths)
+
+
+def gather_around(x, axis, dim):
+    size = lax.axis_size(axis)
+    pairs = [(i, (i + 1) % size) for i in range(size)]
+    back = [(b, a) for a, b in pairs]
+    lower, upper = ([], [])
+    for step in range(size - 1):
+        if step % 2 == 0:
+            lower.append(lax.ppermute(lower[-1] if lower else x, axis, pairs))
+        else:
+            upper.append(lax.ppermute(upper[-1] if upper else x, axis, back))
+    blocks = jnp.stack([*lower[::-1], x, *upper])
+    shift = lax.axis_index(axis) - len(lower)
+    blocks = blocks[(jnp.arange(size) - shift) % size]
+    return joined_along(blocks, dim)
 
 
 def layer_norm(rows, gain):
@@ -75,11 +97,7 @@
     resid = (rows.astype(jnp.float32) + attn).astype(jnp.bfloat16)
     normed_two = layer_norm(resid, ln_mlp).astype(jnp.bfloat16)
     hidden = jax.nn.gelu(
-        jnp.dot(
-            lax.all_gather(normed_two, "req", axis=0, tiled=True),
-            w_up,
-            preferred_element_type=jnp.float32,
-        ),
+        jnp.dot(gather_around(normed_two, "req", 0), w_up, preferred_element_type=jnp.float32),
         approximate=False,
     ).astype(jnp.bfloat16)
     piece = lax.slice_in_dim(hidden, 0, local_rows * lax.axis_size("req"), axis=0)

time: 350 us -> 404 us (1.15)
  starting transfers between devices: 10.5 us -> 48.2 us
  local copies, waits for them, and re-layouts: 4.15 us -> 27 us
  waiting for transfers between devices: 271 us -> 264 us
    all_gather x1 -> x0, waiting for transfers between devices: 55.5 us -> none  [local(): lax.all_gather(normed_two, 'req', axis=0, tiled=True)]
    ppermute x0 -> x15, waiting for transfers between devices: none -> 50.1 us  [the longest x8 49.7 us: gather_around(): lower.append(lax.ppermute(lower[-1] if lower else x, axis, pairs))]
    ppermute x0 -> x15, starting transfers between devices: none -> 39.8 us  [the longest x7 38.5 us: gather_around(): upper.append(lax.ppermute(upper[-1] if upper else x, axis, back))]
    unnamed x17 -> x39, local copies, waits for them, and re-layouts: 1.24 us -> 17.5 us
    gather x0 -> x1, local copies, waits for them, and re-layouts: none -> 5.78 us  [gather_around(): blocks = blocks[(jnp.arange(size) - shift) % size]]
  transfers between devices with their start and end apart: 6 -> 20, of which waited for: 5 -> 13; matrix products, arithmetic and copies ran while one was open for 2% -> 6% of each run, Pallas kernels for 0% -> 0%
where the time goes in v1:
time: 404 us
  waiting for transfers between devices  264 us (65%)
  starting transfers between devices  48.2 us (12%)
  matrix products  37.5 us (9%)
  local copies, waits for them, and re-layouts  27 us (7%)
  between operations  13.4 us (3%)
  other arithmetic  13.3 us (3%)
    reduce_scatter x1, waiting for transfers between devices, local(): lax.psum_scatter(jnp.dot(piece, w_out, preferred_element_type=jnp.float32...  78.7 us
    reduce_scatter x1, waiting for transfers between devices, local(): lax.psum_scatter(jnp.dot(piece, w_down, preferred_element_type=jnp.float3...  70.3 us
    all_gather x1, waiting for transfers between devices, local(): lax.all_gather(normed, 'req', axis=0, tiled=True)  57 us
    ppermute x8, waiting for transfers between devices, gather_around(): lower.append(lax.ppermute(lower[-1] if lower else x, axis, pairs))  49.7 us
    ppermute x7, starting transfers between devices, gather_around(): upper.append(lax.ppermute(upper[-1] if upper else x, axis, back))  38.5 us
    unnamed x39, local copies, waits for them, and re-layouts  17.5 us
    dot_general x1, matrix products, local(): jnp.dot(piece, w_down, preferred_element_type=jnp.float32)  13.4 us
  transfers between devices with their start and end apart: 20, of which 13 were waited for; matrix products, arithmetic and copies ran while one was open for 6% of the time, Pallas kernels for 0%

profile of v1, /device:TPU:0, one launch (start us, length us, event | category | flops | bytes accessed | tf_op | source)
XLA Modules:
  0.0 403.7 jit_solution(7856017601669914221)
XLA Ops:
  12.8 57.0 %all-gather.2.cloned.1.call-done = bf16[2048,1280]{1,0:T(8,128)(2,1)} async-done(((bf16[128,1280]{1,0:T(8,128)(2,1)}), bf16[2048,1280]{1,0:T(8,128)(2,1)}) %all-gather.2.cloned.1.call-update) | async-done | bytes 5242896 | tf_op jit(solution)/shard_map/all_gather | solution.py:63
  75.0 10.9 %while.10 = (s32[]{:T(128)}, bf16[4,512,80]{1,2,0:T(8,128)(2,1)S(1)}, s32[4,512]{1,0:T(4,128)S(1)}, s32[1,2048]{1,0:T(1,128)S(1)}, bf16[4,512,80]{2,1,0:T(8,128)...) while((s32[]{:T(128)}, bf16[4,512,80]{1,2,0:T(8,128)(2,1)S(1)}, ...), condition=%wide.region_8.9_spmd, body=%wide.region_5.8_spmd.sunk | while | flops 345021440 | bytes 13869153 | solution.py:86
  90.0 78.7 %reduce-scatter.3.cloned.1.call-done = bf16[128,1280]{1,0:T(8,128)(2,1)} async-done(((bf16[2048,1280]{1,0:T(8,128)(2,1)}), bf16[128,1280]{1,0:T(8,128)(2,1)}) %reduce-scatter.3.cloned.1.call-update) | async-done | bytes 327696 | tf_op jit(solution)/shard_map/reduce_scatter | solution.py:91
  171.7 10.5 %collective-permute-done = bf16[128,1280]{1,0:T(8,128)(2,1)S(1)} collective-permute-done((bf16[128,1280]{1,0:T(8,128)(2,1)S(1)}, bf16[128,1280]{1,0:T(8,128)(2,1)S(1)}, u32[]{:S(2)}, u32[]{:S(2)}) %collective-permute-start) | collective-permute-done | bytes 327712 | tf_op jit(solution)/shard_map/ppermute | solution.py:23
  182.2 5.3 %collective-permute-start.8 = (bf16[128,1280]{1,0:T(8,128)(2,1)S(1)}, bf16[128,1280]{1,0:T(8,128)(2,1)S(1)}, u32[]{:S(2)}, u32[]{:S(2)}) collective-permute-start(bf16[128,1280]{1,0:T(8,128)(2,1)S(1)} %fusion.58), channel_id=1, source_target_pairs={{8,0},{16,8},{24,16},{32,24},{40,32},{48,40},{56,48},{64,56},{72,6... | collective-permute-start | bytes 983048 | tf_op jit(solution)/shard_map/ppermute | solution.py:25
  187.5 5.4 %collective-permute-done.1 = bf16[128,1280]{1,0:T(8,128)(2,1)S(1)} collective-permute-done((bf16[128,1280]{1,0:T(8,128)(2,1)S(1)}, bf16[128,1280]{1,0:T(8,128)(2,1)S(1)}, u32[]{:S(2)}, u32[]{:S(2)}) %collective-permute-start.1) | collective-permute-done | bytes 327712 | tf_op jit(solution)/shard_map/ppermute | solution.py:23
  192.9 5.3 %collective-permute-start.9 = (bf16[128,1280]{1,0:T(8,128)(2,1)S(1)}, bf16[128,1280]{1,0:T(8,128)(2,1)S(1)}, u32[]{:S(2)}, u32[]{:S(2)}) collective-permute-start(bf16[128,1280]{1,0:T(8,128)(2,1)S(1)} %collective-permute-done.8), channel_id=1, source_target_pairs={{8,0},{16,8},{24,16},{32,24},{40,32},{48,40},{56,48},{64,56},{72,6... | collective-permute-start | bytes 983048 | tf_op jit(solution)/shard_map/ppermute | solution.py:25
  198.3 5.0 %collective-permute-done.2 = bf16[128,1280]{1,0:T(8,128)(2,1)S(1)} collective-permute-done((bf16[128,1280]{1,0:T(8,128)(2,1)S(1)}, bf16[128,1280]{1,0:T(8,128)(2,1)S(1)}, u32[]{:S(2)}, u32[]{:S(2)}) %collective-permute-start.2) | collective-permute-done | bytes 327712 | tf_op jit(solution)/shard_map/ppermute | solution.py:23
  203.3 5.3 %collective-permute-start.10 = (bf16[128,1280]{1,0:T(8,128)(2,1)S(1)}, bf16[128,1280]{1,0:T(8,128)(2,1)S(1)}, u32[]{:S(2)}, u32[]{:S(2)}) collective-permute-start(bf16[128,1280]{1,0:T(8,128)(2,1)S(1)} %collective-permute-done.9), channel_id=1, source_target_pairs={{8,0},{16,8},{24,16},{32,24},{40,32},{48,40},{56,48},{64,56},{72,6... | collective-permute-start | bytes 983048 | tf_op jit(solution)/shard_map/ppermute | solution.py:25
  208.7 5.0 %collective-permute-done.3 = bf16[128,1280]{1,0:T(8,128)(2,1)S(1)} collective-permute-done((bf16[128,1280]{1,0:T(8,128)(2,1)S(1)}, bf16[128,1280]{1,0:T(8,128)(2,1)S(1)}, u32[]{:S(2)}, u32[]{:S(2)}) %collective-permute-start.3) | collective-permute-done | bytes 327712 | tf_op jit(solution)/shard_map/ppermute | solution.py:23
  213.7 5.3 %collective-permute-start.11 = (bf16[128,1280]{1,0:T(8,128)(2,1)S(1)}, bf16[128,1280]{1,0:T(8,128)(2,1)S(1)}, u32[]{:S(2)}, u32[]{:S(2)}) collective-permute-start(bf16[128,1280]{1,0:T(8,128)(2,1)S(1)} %collective-permute-done.10), channel_id=1, source_target_pairs={{8,0},{16,8},{24,16},{32,24},{40,32},{48,40},{56,48},{64,56},{72,6... | collective-permute-start | bytes 983048 | tf_op jit(solution)/shard_map/ppermute | solution.py:25
  219.1 5.6 %collective-permute-done.4 = bf16[128,1280]{1,0:T(8,128)(2,1)S(1)} collective-permute-done((bf16[128,1280]{1,0:T(8,128)(2,1)S(1)}, bf16[128,1280]{1,0:T(8,128)(2,1)S(1)}, u32[]{:S(2)}, u32[]{:S(2)}) %collective-permute-start.4) | collective-permute-done | bytes 327712 | tf_op jit(solution)/shard_map/ppermute | solution.py:23
  224.7 5.6 %collective-permute-start.12 = (bf16[128,1280]{1,0:T(8,128)(2,1)S(1)}, bf16[128,1280]{1,0:T(8,128)(2,1)}, u32[]{:S(2)}, u32[]{:S(2)}) collective-permute-start(bf16[128,1280]{1,0:T(8,128)(2,1)S(1)} %collective-permute-done.11), channel_id=1, source_target_pairs={{8,0},{16,8},{24,16},{32,24},{40,32},{48,40},{56,48},{64,56},{72,6... | collective-permute-start | bytes 983048 | tf_op jit(solution)/shard_map/ppermute | solution.py:25
  230.3 6.4 %collective-permute-done.5 = bf16[128,1280]{1,0:T(8,128)(2,1)S(1)} collective-permute-done((bf16[128,1280]{1,0:T(8,128)(2,1)S(1)}, bf16[128,1280]{1,0:T(8,128)(2,1)S(1)}, u32[]{:S(2)}, u32[]{:S(2)}) %collective-permute-start.5) | collective-permute-done | bytes 327712 | tf_op jit(solution)/shard_map/ppermute | solution.py:23
  236.7 5.7 %collective-permute-start.13 = (bf16[128,1280]{1,0:T(8,128)(2,1)}, bf16[128,1280]{1,0:T(8,128)(2,1)}, u32[]{:S(2)}, u32[]{:S(2)}) collective-permute-start(bf16[128,1280]{1,0:T(8,128)(2,1)} %collective-permute-done.12), channel_id=1, source_target_pairs={{8,0},{16,8},{24,16},{32,24},{40,32},{48,40},{56,48},{64,56},{72,6... | collective-permute-start | bytes 983048 | tf_op jit(solution)/shard_map/ppermute | solution.py:25
  242.4 7.2 %collective-permute-done.6 = bf16[128,1280]{1,0:T(8,128)(2,1)} collective-permute-done((bf16[128,1280]{1,0:T(8,128)(2,1)S(1)}, bf16[128,1280]{1,0:T(8,128)(2,1)}, u32[]{:S(2)}, u32[]{:S(2)}) %collective-permute-start.6) | collective-permute-done | bytes 327712 | tf_op jit(solution)/shard_map/ppermute | solution.py:23
  250.1 5.8 %collective-permute-start.14 = (bf16[128,1280]{1,0:T(8,128)(2,1)}, bf16[128,1280]{1,0:T(8,128)(2,1)S(1)}, u32[]{:S(2)}, u32[]{:S(2)}) collective-permute-start(bf16[128,1280]{1,0:T(8,128)(2,1)} %collective-permute-done.13), channel_id=1, source_target_pairs={{8,0},{16,8},{24,16},{32,24},{40,32},{48,40},{56,48},{64,56},{72,6... | collective-permute-start | bytes 983048 | tf_op jit(solution)/shard_map/ppermute | solution.py:25
  255.9 4.5 %collective-permute-done.7 = bf16[128,1280]{1,0:T(8,128)(2,1)} collective-permute-done((bf16[128,1280]{1,0:T(8,128)(2,1)}, bf16[128,1280]{1,0:T(8,128)(2,1)}, u32[]{:S(2)}, u32[]{:S(2)}) %collective-permute-start.7) | collective-permute-done | bytes 327712 | tf_op jit(solution)/shard_map/ppermute | solution.py:23
  278.4 5.8 %gather_fusion = bf16[16,128,1280]{2,1,0:T(8,128)(2,1)} fusion(bf16[16,128,1280]{2,1,0:T(8,128)(2,1)} %bitcast_dynamic-update-slice_fusion, s32[1024]{0:T(1024)S(1)} %pad_clamp_fusion), kind=kCustom, calls=%fused_computation | custom fusion | bytes 10485824 | tf_op jit(solution)/shard_map/gather | solution.py:28
  284.2 13.4 %convolution_convert_fusion = bf16[2048,1280]{1,0:T(8,128)(2,1)} fusion(bf16[320,1280]{1,0:T(8,128)(2,1)S(1)} %copy-done, bf16[2048,1280]{1,0:T(8,128)(2,1)} %bitcast.123, bf16[1280,320]{0,1:T(8,128)(2,1)S(1)} %copy-done.10), kind=kOutput, calls=%fused_computation.13 | convolution fusion | flops 3400663040 | bytes 12124160 | tf_op jit(solution)/shard_map/dot_general | solution.py:105
  302.7 70.3 %reduce-scatter.5.cloned.1.call-done = bf16[128,1280]{1,0:T(8,128)(2,1)} async-done(((bf16[2048,1280]{1,0:T(8,128)(2,1)}), bf16[128,1280]{1,0:T(8,128)(2,1)}) %reduce-scatter.5.cloned.1.call-update) | async-done | bytes 327696 | tf_op jit(solution)/shard_map/reduce_scatter | solution.py:104
  375.3 4.9 %all-to-all-start.1 = ((bf16[16,2,5120]{2,1,0:T(2,128)(2,1)}), bf16[16,2,5120]{2,1,0:T(2,128)(2,1)S(1)}, u32[]{:S(2)}, u32[]{:S(2)}) async-start(bf16[16,2,5120]{2,1,0:T(2,128)(2,1)} %reshape.166), calls=%async_computation.3 | async-start | bytes 655360 | tf_op jit(solution)/shard_map/all_to_all | solution.py:126
  381.0 8.1 %all-to-all-done.1 = bf16[16,2,5120]{2,1,0:T(2,128)(2,1)S(1)} async-done(((bf16[16,2,5120]{2,1,0:T(2,128)(2,1)}), bf16[16,2,5120]{2,1,0:T(2,128)(2,1)S(1)}, u32[]{:S(2)}, u32[]{:S(2)}) %all-to-all-start.1) | async-done | bytes 327712 | tf_op jit(solution)/shard_map/all_to_all | solution.py:126
  389.2 7.9 %fusion.18 = bf16[128,1280]{1,0:T(8,128)(2,1)} fusion(bf16[128,1280]{1,0:T(8,128)(2,1)S(1)} %copy-done.2, bf16[32,5120]{1,0:T(8,128)(2,1)S(1)} %reshape.167, bf16[5120,1280]{1,0:T(8,128)(2,1)} %param.21, pred[128]{0:T(512)(128)(4,1)S(1)} %fusion.64, s32[32]{0:T(128)S(1)} %eq.71), kind=kOutput, calls=%fused_computation.36 | convolution fusion | flops 430288896 | bytes 14090496 | tf_op jit(solution)/shard_map/dot_general | solution.py:141
  (118 shorter events, 56.0 us)
Async XLA Ops:
  6.5 277.7 %copy-start = (bf16[320,1280]{1,0:T(8,128)(2,1)S(1)}, bf16[320,1280]{1,0:T(8,128)(2,1)}, u32[]{:S(2)}) copy-start(bf16[320,1280]{1,0:T(8,128)(2,1)} %param.20) | copy-start | bytes 2457604
  6.5 63.2 %all-gather.2.cloned.1.call-start = ((), (), s32[]{:S(2)}) async-start(), calls=%async_computation.4 | async-start | bytes 5570560 | tf_op jit(solution)/shard_map/all_gather | solution.py:63
  10.9 157.8 %reduce-scatter.3.cloned.1.call-start = ((), (), s32[]{:S(2)}) async-start(), calls=%async_computation.5 | async-start | bytes 5570560 | tf_op jit(solution)/shard_map/reduce_scatter | solution.py:91
  89.9 78.8 %copy-start.1 = (bf16[1,128,1280]{2,1,0:T(8,128)(2,1)S(1)}, bf16[1,128,1280]{2,1,0:T(8,128)(2,1)}, u32[]{:S(2)}) copy-start(bf16[1,128,1280]{2,1,0:T(8,128)(2,1)} %param.13) | copy-start | bytes 983044
  89.9 80.2 %copy-start.8 = (f32[1280]{0:T(1024)S(1)}, f32[1280]{0:T(1024)}, u32[]{:S(2)}) copy-start(f32[1280]{0:T(1024)} %param.18) | copy-start | bytes 15364
  89.9 283.1 %reduce-scatter.5.cloned.1.call-start = ((), (), s32[]{:S(2)}) async-start(), calls=%async_computation.6 | async-start | bytes 5570560 | tf_op jit(solution)/shard_map/reduce_scatter | solution.py:104
  170.4 11.8 %collective-permute-start = (bf16[128,1280]{1,0:T(8,128)(2,1)S(1)}, bf16[128,1280]{1,0:T(8,128)(2,1)S(1)}, u32[]{:S(2)}, u32[]{:S(2)}) collective-permute-start(bf16[128,1280]{1,0:T(8,128)(2,1)S(1)} %fusion.58), channel_id=1, source_target_pairs={{0,8},{8,16},{16,24},{24,32},{32,40},{40,48},{48,56},{56,64},{64,7... | collective-permute-start | bytes 983048 | tf_op jit(solution)/shard_map/ppermute | solution.py:23
  182.2 10.8 %collective-permute-start.1 = (bf16[128,1280]{1,0:T(8,128)(2,1)S(1)}, bf16[128,1280]{1,0:T(8,128)(2,1)S(1)}, u32[]{:S(2)}, u32[]{:S(2)}) collective-permute-start(bf16[128,1280]{1,0:T(8,128)(2,1)S(1)} %collective-permute-done), channel_id=1, source_target_pairs={{0,8},{8,16},{16,24},{24,32},{32,40},{40,48},{48,56},{56,64},{64,7... | collective-permute-start | bytes 983048 | tf_op jit(solution)/shard_map/ppermute | solution.py:23
  182.2 10.8 %collective-permute-start.8 = (bf16[128,1280]{1,0:T(8,128)(2,1)S(1)}, bf16[128,1280]{1,0:T(8,128)(2,1)S(1)}, u32[]{:S(2)}, u32[]{:S(2)}) collective-permute-start(bf16[128,1280]{1,0:T(8,128)(2,1)S(1)} %fusion.58), channel_id=1, source_target_pairs={{8,0},{16,8},{24,16},{32,24},{40,32},{48,40},{56,48},{64,56},{72,6... | collective-permute-start | bytes 983048 | tf_op jit(solution)/shard_map/ppermute | solution.py:25
  192.9 10.4 %collective-permute-start.2 = (bf16[128,1280]{1,0:T(8,128)(2,1)S(1)}, bf16[128,1280]{1,0:T(8,128)(2,1)S(1)}, u32[]{:S(2)}, u32[]{:S(2)}) collective-permute-start(bf16[128,1280]{1,0:T(8,128)(2,1)S(1)} %collective-permute-done.1), channel_id=1, source_target_pairs={{0,8},{8,16},{16,24},{24,32},{32,40},{40,48},{48,56},{56,64},{64,7... | collective-permute-start | bytes 983048 | tf_op jit(solution)/shard_map/ppermute | solution.py:23
  192.9 10.4 %collective-permute-start.9 = (bf16[128,1280]{1,0:T(8,128)(2,1)S(1)}, bf16[128,1280]{1,0:T(8,128)(2,1)S(1)}, u32[]{:S(2)}, u32[]{:S(2)}) collective-permute-start(bf16[128,1280]{1,0:T(8,128)(2,1)S(1)} %collective-permute-done.8), channel_id=1, source_target_pairs={{8,0},{16,8},{24,16},{32,24},{40,32},{48,40},{56,48},{64,56},{72,6... | collective-permute-start | bytes 983048 | tf_op jit(solution)/shard_map/ppermute | solution.py:25
  203.3 10.4 %collective-permute-start.3 = (bf16[128,1280]{1,0:T(8,128)(2,1)S(1)}, bf16[128,1280]{1,0:T(8,128)(2,1)S(1)}, u32[]{:S(2)}, u32[]{:S(2)}) collective-permute-start(bf16[128,1280]{1,0:T(8,128)(2,1)S(1)} %collective-permute-done.2), channel_id=1, source_target_pairs={{0,8},{8,16},{16,24},{24,32},{32,40},{40,48},{48,56},{56,64},{64,7... | collective-permute-start | bytes 983048 | tf_op jit(solution)/shard_map/ppermute | solution.py:23
  203.3 10.4 %collective-permute-start.10 = (bf16[128,1280]{1,0:T(8,128)(2,1)S(1)}, bf16[128,1280]{1,0:T(8,128)(2,1)S(1)}, u32[]{:S(2)}, u32[]{:S(2)}) collective-permute-start(bf16[128,1280]{1,0:T(8,128)(2,1)S(1)} %collective-permute-done.9), channel_id=1, source_target_pairs={{8,0},{16,8},{24,16},{32,24},{40,32},{48,40},{56,48},{64,56},{72,6... | collective-permute-start | bytes 983048 | tf_op jit(solution)/shard_map/ppermute | solution.py:25
  213.7 10.9 %collective-permute-start.4 = (bf16[128,1280]{1,0:T(8,128)(2,1)S(1)}, bf16[128,1280]{1,0:T(8,128)(2,1)S(1)}, u32[]{:S(2)}, u32[]{:S(2)}) collective-permute-start(bf16[128,1280]{1,0:T(8,128)(2,1)S(1)} %collective-permute-done.3), channel_id=1, source_target_pairs={{0,8},{8,16},{16,24},{24,32},{32,40},{40,48},{48,56},{56,64},{64,7... | collective-permute-start | bytes 983048 | tf_op jit(solution)/shard_map/ppermute | solution.py:23
  213.7 10.9 %collective-permute-start.11 = (bf16[128,1280]{1,0:T(8,128)(2,1)S(1)}, bf16[128,1280]{1,0:T(8,128)(2,1)S(1)}, u32[]{:S(2)}, u32[]{:S(2)}) collective-permute-start(bf16[128,1280]{1,0:T(8,128)(2,1)S(1)} %collective-permute-done.10), channel_id=1, source_target_pairs={{8,0},{16,8},{24,16},{32,24},{40,32},{48,40},{56,48},{64,56},{72,6... | collective-permute-start | bytes 983048 | tf_op jit(solution)/shard_map/ppermute | solution.py:25
  224.7 12.0 %collective-permute-start.5 = (bf16[128,1280]{1,0:T(8,128)(2,1)S(1)}, bf16[128,1280]{1,0:T(8,128)(2,1)S(1)}, u32[]{:S(2)}, u32[]{:S(2)}) collective-permute-start(bf16[128,1280]{1,0:T(8,128)(2,1)S(1)} %collective-permute-done.4), channel_id=1, source_target_pairs={{0,8},{8,16},{16,24},{24,32},{32,40},{40,48},{48,56},{56,64},{64,7... | collective-permute-start | bytes 983048 | tf_op jit(solution)/shard_map/ppermute | solution.py:23
  224.7 12.0 %collective-permute-start.12 = (bf16[128,1280]{1,0:T(8,128)(2,1)S(1)}, bf16[128,1280]{1,0:T(8,128)(2,1)}, u32[]{:S(2)}, u32[]{:S(2)}) collective-permute-start(bf16[128,1280]{1,0:T(8,128)(2,1)S(1)} %collective-permute-done.11), channel_id=1, source_target_pairs={{8,0},{16,8},{24,16},{32,24},{40,32},{48,40},{56,48},{64,56},{72,6... | collective-permute-start | bytes 983048 | tf_op jit(solution)/shard_map/ppermute | solution.py:25
  236.7 12.9 %collective-permute-start.6 = (bf16[128,1280]{1,0:T(8,128)(2,1)S(1)}, bf16[128,1280]{1,0:T(8,128)(2,1)}, u32[]{:S(2)}, u32[]{:S(2)}) collective-permute-start(bf16[128,1280]{1,0:T(8,128)(2,1)S(1)} %collective-permute-done.5), channel_id=1, source_target_pairs={{0,8},{8,16},{16,24},{24,32},{32,40},{40,48},{48,56},{56,64},{64,7... | collective-permute-start | bytes 983048 | tf_op jit(solution)/shard_map/ppermute | solution.py:23
  236.7 13.4 %collective-permute-start.13 = (bf16[128,1280]{1,0:T(8,128)(2,1)}, bf16[128,1280]{1,0:T(8,128)(2,1)}, u32[]{:S(2)}, u32[]{:S(2)}) collective-permute-start(bf16[128,1280]{1,0:T(8,128)(2,1)} %collective-permute-done.12), channel_id=1, source_target_pairs={{8,0},{16,8},{24,16},{32,24},{40,32},{48,40},{56,48},{64,56},{72,6... | collective-permute-start | bytes 983048 | tf_op jit(solution)/shard_map/ppermute | solution.py:25
  249.6 10.7 %collective-permute-start.7 = (bf16[128,1280]{1,0:T(8,128)(2,1)}, bf16[128,1280]{1,0:T(8,128)(2,1)}, u32[]{:S(2)}, u32[]{:S(2)}) collective-permute-start(bf16[128,1280]{1,0:T(8,128)(2,1)} %collective-permute-done.6), channel_id=1, source_target_pairs={{0,8},{8,16},{16,24},{24,32},{32,40},{40,48},{48,56},{56,64},{64,7... | collective-permute-start | bytes 983048 | tf_op jit(solution)/shard_map/ppermute | solution.py:23
  250.1 27.6 %collective-permute-start.14 = (bf16[128,1280]{1,0:T(8,128)(2,1)}, bf16[128,1280]{1,0:T(8,128)(2,1)S(1)}, u32[]{:S(2)}, u32[]{:S(2)}) collective-permute-start(bf16[128,1280]{1,0:T(8,128)(2,1)} %collective-permute-done.13), channel_id=1, source_target_pairs={{8,0},{16,8},{24,16},{32,24},{40,32},{48,40},{56,48},{64,56},{72,6... | collective-permute-start | bytes 983048 | tf_op jit(solution)/shard_map/ppermute | solution.py:25
  298.2 91.0 %copy-start.2 = (bf16[128,1280]{1,0:T(8,128)(2,1)S(1)}, bf16[128,1280]{1,0:T(8,128)(2,1)}, u32[]{:S(2)}) copy-start(bf16[128,1280]{1,0:T(8,128)(2,1)} %param.22) | copy-start | bytes 983044
  299.3 76.1 %all-to-all-start = ((s32[16,1,2]{2,1,0:T(1,128)}), s32[16,1,2]{2,1,0:T(1,128)S(1)}, u32[]{:S(2)}, u32[]{:S(2)}) async-start(s32[16,1,2]{2,1,0:T(1,128)} %bitcast.9), calls=%async_computation | async-start | bytes 16384 | tf_op jit(solution)/shard_map/all_to_all | solution.py:133
  375.3 13.7 %all-to-all-start.1 = ((bf16[16,2,5120]{2,1,0:T(2,128)(2,1)}), bf16[16,2,5120]{2,1,0:T(2,128)(2,1)S(1)}, u32[]{:S(2)}, u32[]{:S(2)}) async-start(bf16[16,2,5120]{2,1,0:T(2,128)(2,1)} %reshape.166), calls=%async_computation.3 | async-start | bytes 655360 | tf_op jit(solution)/shard_map/all_to_all | solution.py:126
  (8 other events, 89.6 us)
Sparse Core Ops, SparseCore 0:
  11.0 58.7 all-gather.1
  90.0 78.6 reduce-scatter.2
  297.7 75.2 reduce-scatter.4
